TPU v7x, 32 devices: a whole 2x2x4 slice. The times are simulated.
32 devices in a mesh: batch: 4 (over z), seq: 2 (over core), ch: 4 (over y, x).
Axes of the slice: x: 2, y: 2, z: 4, core: 2. Of those that a mesh axis runs over, the one named last changes fastest.
Arguments:
- inputs: bfloat16 [16, 1280, 2048], P('batch', 'ch', 'seq'), may hold values from -6 to 6
- segment_ids: int32 [16, 2048], P('batch', 'seq'), may hold values from 0 to 7, never falling along the last dimension, each value on 1 to 512 neighbouring positions
- norm0_gain: float32 [1280], P('ch'), may hold values from 0.1 to 1.9
- norm0_shift: float32 [1280], P('ch'), may hold values from -3 to 3
- w_inner: bfloat16 [1280, 640], P('ch'), may hold values from -0.15625 to 0.15625
- b_inner: float32 [640], P('ch'), may hold values from -3 to 3
- norm1_gain: float32 [640], P('ch'), may hold values from 0.1 to 1.9
- norm1_shift: float32 [640], P('ch'), may hold values from -3 to 3
- w_conv: bfloat16 [5, 640, 640], P(None, 'ch'), may hold values from -0.109375 to 0.109375
- b_conv: float32 [640], P('ch'), may hold values from -3 to 3
- norm2_gain: float32 [640], P('ch'), may hold values from 0.1 to 1.9
- norm2_shift: float32 [640], P('ch'), may hold values from -3 to 3
- w_outer: bfloat16 [640, 1280], P('ch'), may hold values from -0.25 to 0.25
- b_outer: float32 [1280], P('ch'), may hold values from -3 to 3
- cotangent: bfloat16 [16, 1280, 2048], P('batch', 'ch', 'seq'), may hold values from -6 to 6
Outputs:
- output: bfloat16 [16, 1280, 2048], P('batch', 'ch', 'seq')
- input_grad: bfloat16 [16, 1280, 2048], P('batch', 'ch', 'seq')
- grad_norm0_gain: float32 [1280], P('ch')
- grad_norm0_shift: float32 [1280], P('ch')
- grad_w_inner: float32 [1280, 640], P('ch')
- grad_b_inner: float32 [640], P('ch')
- grad_norm1_gain: float32 [640], P('ch')
- grad_norm1_shift: float32 [640], P('ch')
- grad_w_conv: float32 [5, 640, 640], P(None, 'ch')
- grad_b_conv: float32 [640], P('ch')
- grad_norm2_gain: float32 [640], P('ch')
- grad_norm2_shift: float32 [640], P('ch')
- grad_w_outer: float32 [640, 1280], P('ch')
- grad_b_outer: float32 [1280], P('ch')
Inputs may be any that keep to these rules, and one draw needn't show every extreme that they name: `segment_ids`: along a row the ids never fall; each protein is one run of 1 to 512 residues, one run of each row has exactly 512, and every row holds all 8 ids.
All inputs are finite; a program needn't handle non-finite values.
Results may differ from a plain program's by a relative error of at most 0.0065.
Values may be sent and summed in bfloat16 or wider, within the bound.
A program may use at most 192 MiB of HBM per device.

v0:
```python
import jax
import jax.numpy as jnp
from jax import lax
from jax.sharding import PartitionSpec as P

KERNEL_TAPS = 5
DILATION_SPACING = 32
EPSILON = 1e-05


def extended(x, sides, width):
    for axis, dim in sides:
        size, length = (lax.axis_size(axis), x.shape[dim])
        up = [(i, (i + 1) % size) for i in range(size - 1)]
        down = [(j, i) for i, j in up]
        last = lax.slice_in_dim(x, length - width, length, axis=dim)
        leading = lax.slice_in_dim(x, 0, width, axis=dim)
        before = lax.ppermute(last, axis, up)
        after = lax.ppermute(leading, axis, down)
        x = jnp.concatenate([before, x, after], axis=dim)
    return x


def gelu_exact(values):
    return jax.nn.gelu(values, approximate=False)


def gelu_back(point, grad):
    return jax.vjp(gelu_exact, point)[1](grad)[0]


def channel_sums(first, second):
    return lax.psum((first, second), "ch")


def normalize(values, gain, shift):
    width = values.shape[1] * lax.axis_size("ch")
    total, squares = channel_sums(
        jnp.sum(values, axis=1, keepdims=True), jnp.sum(values * values, axis=1, keepdims=True)
    )
    center = total / width
    spread = squares / width - center * center
    scale = lax.rsqrt(spread + EPSILON)
    unit = (values - center) * scale
    return (unit * gain[:, None] + shift[:, None], unit, scale)


def normalize_back(grad, unit, scale, gain):
    width = grad.shape[1] * lax.axis_size("ch")
    scaled = grad * gain[:, None]
    first, second = channel_sums(
        jnp.sum(scaled, axis=1, keepdims=True), jnp.sum(scaled * unit, axis=1, keepdims=True)
    )
    return scale * (scaled - first / width - unit * (second / width))


def shifted_taps(wide, wide_ids, own_ids, tap_displacements, border_extent):
    length = own_ids.shape[1]
    pieces = []
    for tap_displacement in tap_displacements:
        lower = border_extent + tap_displacement
        shifted = wide[:, :, lower : lower + length]
        matching = wide_ids[:, lower : lower + length] == own_ids
        pieces.append(jnp.where(matching[:, None, :], shifted, jnp.zeros_like(shifted)))
    return jnp.stack(pieces, axis=1)


def local(
    inputs,
    segment_ids,
    norm0_gain,
    norm0_shift,
    w_inner,
    b_inner,
    norm1_gain,
    norm1_shift,
    w_conv,
    b_conv,
    norm2_gain,
    norm2_shift,
    w_outer,
    b_outer,
    cotangent,
):
    border_extent = 2 * DILATION_SPACING
    tap_displacements = [
        (tap_stride - KERNEL_TAPS // 2) * DILATION_SPACING for tap_stride in range(KERNEL_TAPS)
    ]
    back_offsets = [-tap_displacement for tap_displacement in tap_displacements]
    residual = inputs.astype(jnp.float32)
    normed0, unit0, scale0 = normalize(residual, norm0_gain, norm0_shift)
    hidden0 = gelu_exact(normed0).astype(jnp.bfloat16)
    inner_terms = jnp.einsum("sdl,dh->shl", hidden0, w_inner, preferred_element_type=jnp.float32)
    inner = lax.psum_scatter(inner_terms, "ch", scatter_dimension=1, tiled=True) + b_inner[:, None]
    normed1, unit1, scale1 = normalize(inner, norm1_gain, norm1_shift)
    hidden1 = gelu_exact(normed1).astype(jnp.bfloat16)
    own_ids = segment_ids + 1
    wide_ids = extended(own_ids, (("seq", 1),), border_extent)
    wide_hidden = extended(hidden1, (("seq", 2),), border_extent)
    taps = shifted_taps(wide_hidden, wide_ids, own_ids, tap_displacements, border_extent)
    seqs, width, length = hidden1.shape
    taps_flat = taps.reshape(seqs, KERNEL_TAPS * width, length)
    kernel_flat = w_conv.reshape(KERNEL_TAPS * width, w_conv.shape[2])
    conv_terms = jnp.einsum(
        "scl,ch->shl", taps_flat, kernel_flat, preferred_element_type=jnp.float32
    )
    mixed = lax.psum_scatter(conv_terms, "ch", scatter_dimension=1, tiled=True) + b_conv[:, None]
    normed2, unit2, scale2 = normalize(mixed, norm2_gain, norm2_shift)
    hidden2 = gelu_exact(normed2).astype(jnp.bfloat16)
    outer_terms = jnp.einsum("shl,hd->sdl", hidden2, w_outer, preferred_element_type=jnp.float32)
    branch = lax.psum_scatter(outer_terms, "ch", scatter_dimension=1, tiled=True)
    output = (residual + branch + b_outer[:, None]).astype(jnp.bfloat16)
    piece = lax.all_gather(cotangent, "ch", axis=1, tiled=True)
    block = w_outer
    hidden_gradient = jnp.einsum("snl,hn->shl", piece, block, preferred_element_type=jnp.float32)
    part = jnp.einsum("shl,snl->hn", hidden2, piece, preferred_element_type=jnp.float32)
    grad_weight = part
    grad_hidden2 = hidden_gradient
    grad_w_outer = grad_weight
    grad_b_outer = jnp.sum(cotangent.astype(jnp.float32), axis=(0, 2))
    grad_normed2 = gelu_back(normed2, grad_hidden2)
    grad_norm2_gain = jnp.sum(grad_normed2 * unit2, axis=(0, 2))
    grad_norm2_shift = jnp.sum(grad_normed2, axis=(0, 2))
    grad_mixed = normalize_back(grad_normed2, unit2, scale2, norm2_gain).astype(jnp.bfloat16)
    grad_b_conv = jnp.sum(grad_mixed.astype(jnp.float32), axis=(0, 2))
    wide_grad = extended(grad_mixed, (("seq", 2),), border_extent)
    piece = lax.all_gather(wide_grad, "ch", axis=1, tiled=True)
    count = piece.shape[1]
    back_taps = shifted_taps(piece, wide_ids, own_ids, back_offsets, border_extent)
    back_flat = back_taps.reshape(seqs, KERNEL_TAPS * count, length)
    kernel_back = jnp.transpose(w_conv, (0, 2, 1)).reshape(KERNEL_TAPS * count, width)
    hidden_gradient = jnp.einsum(
        "sml,mc->scl", back_flat, kernel_back, preferred_element_type=jnp.float32
    )
    center = piece[:, :, border_extent : border_extent + length]
    part = jnp.einsum("sml,snl->mn", taps_flat, center, preferred_element_type=jnp.float32).reshape(
        KERNEL_TAPS, width, count
    )
    grad_kernel = part
    grad_hidden1 = hidden_gradient
    grad_normed1 = gelu_back(normed1, grad_hidden1)
    grad_norm1_gain = jnp.sum(grad_normed1 * unit1, axis=(0, 2))
    grad_norm1_shift = jnp.sum(grad_normed1, axis=(0, 2))
    grad_inner = normalize_back(grad_normed1, unit1, scale1, norm1_gain).astype(jnp.bfloat16)
    grad_b_inner = jnp.sum(grad_inner.astype(jnp.float32), axis=(0, 2))
    piece = lax.all_gather(grad_inner, "ch", axis=1, tiled=True)
    block = w_inner
    hidden_gradient = jnp.einsum("snl,dn->sdl", piece, block, preferred_element_type=jnp.float32)
    part = jnp.einsum("sdl,snl->dn", hidden0, piece, preferred_element_type=jnp.float32)
    grad_weight = part
    grad_normed0 = gelu_back(normed0, hidden_gradient)
    grad_norm0_gain = jnp.sum(grad_normed0 * unit0, axis=(0, 2))
    grad_norm0_shift = jnp.sum(grad_normed0, axis=(0, 2))
    input_grad = (
        cotangent.astype(jnp.float32) + normalize_back(grad_normed0, unit0, scale0, norm0_gain)
    ).astype(jnp.bfloat16)
    totals = lax.psum(
        (
            grad_norm0_gain,
            grad_norm0_shift,
            grad_weight,
            grad_b_inner,
            grad_norm1_gain,
            grad_norm1_shift,
            grad_kernel,
            grad_b_conv,
            grad_norm2_gain,
            grad_norm2_shift,
            grad_w_outer,
            grad_b_outer,
        ),
        ("batch", "seq"),
    )
    return (
        output,
        input_grad,
        totals[0],
        totals[1],
        totals[2],
        totals[3],
        totals[4],
        totals[5],
        totals[6],
        totals[7],
        totals[8],
        totals[9],
        totals[10],
        totals[11],
    )


def solution(mesh):
    return jax.shard_map(
        local,
        mesh=mesh,
        in_specs=(
            P("batch", "ch", "seq"),
            P("batch", "seq"),
            P("ch"),
            P("ch"),
            P("ch", None),
            P("ch"),
            P("ch"),
            P("ch"),
            P(None, "ch", None),
            P("ch"),
            P("ch"),
            P("ch"),
            P("ch", None),
            P("ch"),
            P("batch", "ch", "seq"),
        ),
        out_specs=(
            P("batch", "ch", "seq"),
            P("batch", "ch", "seq"),
            P("ch"),
            P("ch"),
            P("ch", None),
            P("ch"),
            P("ch"),
            P("ch"),
            P(None, "ch", None),
            P("ch"),
            P("ch"),
            P("ch"),
            P("ch", None),
            P("ch"),
        ),
        check_vma=False,
    )
```

profile of v0, /device:TPU:0, one launch (start us, length us, event | category | flops | bytes accessed | tf_op | source)
XLA Modules:
  0.0 1400.8 jit_solution(3146654529673238040)
XLA Ops:
  9.8 17.8 %all-reduce.10 = (f32[4,1,1024]{2,0,1:T(4,128)S(1)}, f32[4,1,1024]{2,0,1:T(4,128)S(1)}) all-reduce(f32[4,1,1024]{2,0,1:T(4,128)S(1)} %bitcast.197, f32[4,1,1024]{2,0,1:T(4,128)S(1)} %bitcast.196), channel_id=1, replica_groups=mesh['batch'=4,'seq'=2,'ch'=4] {'ch'}, use_global_device_ids=true, to_apply=%region_3.0 | all-reduce | flops 8192 | bytes 65536 | tf_op jit(solution)/shard_map/psum | solution.py:33
  27.7 14.6 %multiply_convert_fusion = (bf16[4,320,1024]{2,1,0:T(8,128)(2,1)S(1)}, f32[4,320,1024]{2,1,0:T(8,128)}) fusion(bf16[4,320,1024]{2,1,0:T(8,128)(2,1)} %param.15, f32[320]{0:T(512)S(1)} %copy-done.34, f32[320]{0:T(512)S(1)} %copy-done.28, f32[4,1024]{1,0:T(4,128)S(1)} %get-tuple-element.117, f32[4,1024]{1,0:T(4,128)S(1)} %get-tuple-element.116), kind=kLoop, calls=%fused_computation.51 | loop fusion | flops 91750400 | bytes 10521088 | tf_op jit(solution)/shard_map/convert_element_type | solution.py:92
  43.8 5.7 convolution_bitcast_fusion.1
  49.6 12.9 copy.63
  68.8 199.4 %all-reduce.16.cloned.1.call-done = f32[4,640,1024]{2,0,1:T(4,128)} async-done(((f32[4,640,1024]{2,0,1:T(4,128)}), f32[4,640,1024]{2,0,1:T(4,128)}) %all-reduce.16.cloned.1.call-update) | async-done | bytes 10485776
  273.6 15.7 %all-reduce.9 = (f32[4,1,1024]{2,0,1:T(4,128)S(1)}, f32[4,1,1024]{2,0,1:T(4,128)S(1)}) all-reduce(f32[4,1,1024]{2,0,1:T(4,128)S(1)} %bitcast.193, f32[4,1,1024]{2,0,1:T(4,128)S(1)} %bitcast.192), channel_id=1, replica_groups=mesh['batch'=4,'seq'=2,'ch'=4] {'ch'}, use_global_device_ids=true, to_apply=%region_8.0 | all-reduce | flops 8192 | bytes 65536 | tf_op jit(solution)/shard_map/psum | solution.py:33
  289.3 8.2 multiply_convert_fusion.4
  302.3 7.1 bitcast_dynamic-update-slice_fusion.1
  313.8 9.1 convolution_bitcast_fusion.2
  322.9 12.9 copy.65
  336.6 206.1 %all-reduce.18.cloned.1.call-done = f32[4,640,1024]{2,0,1:T(4,128)} async-done(((f32[4,640,1024]{2,0,1:T(4,128)}), f32[4,640,1024]{2,0,1:T(4,128)}) %all-reduce.18.cloned.1.call-update) | async-done | bytes 10485776
  547.9 16.7 %all-reduce.8 = (f32[4,1,1024]{2,0,1:T(4,128)S(1)}, f32[4,1,1024]{2,0,1:T(4,128)S(1)}) all-reduce(f32[4,1,1024]{2,0,1:T(4,128)S(1)} %bitcast.195, f32[4,1,1024]{2,0,1:T(4,128)S(1)} %bitcast.194), channel_id=1, replica_groups=mesh['batch'=4,'seq'=2,'ch'=4] {'ch'}, use_global_device_ids=true, to_apply=%region_13.14 | all-reduce | flops 8192 | bytes 65536 | tf_op jit(solution)/shard_map/psum | solution.py:33
  564.7 9.1 multiply_convert_fusion.3
  573.8 76.4 %all-gather.4.cloned.1.call-done = bf16[4,1280,1024]{2,1,0:T(8,128)(2,1)} async-done(((bf16[4,320,1024]{2,1,0:T(8,128)(2,1)}), bf16[4,1280,1024]{2,1,0:T(8,128)(2,1)}) %all-gather.4.cloned.1.call-update) | async-done | bytes 10485776 | tf_op jit(solution)/shard_map/all_gather | solution.py:113
  650.2 12.3 multiply_reduce_fusion.1
  662.5 15.3 %all-reduce.7 = (f32[4,1,1024]{2,0,1:T(4,128)S(1)}, f32[4,1,1024]{2,0,1:T(4,128)S(1)}) all-reduce(f32[4,1,1024]{2,0,1:T(4,128)S(1)} %bitcast.200, f32[4,1,1024]{2,0,1:T(4,128)S(1)} %bitcast.201), channel_id=1, replica_groups=mesh['batch'=4,'seq'=2,'ch'=4] {'ch'}, use_global_device_ids=true, to_apply=%region_18.19 | all-reduce | flops 8192 | bytes 65536 | tf_op jit(solution)/shard_map/psum | solution.py:33
  694.9 66.8 %all-gather.6.cloned.1.call-done = bf16[4,640,1152]{2,0,1:T(4,128)(2,1)} async-done(((bf16[4,160,1152]{2,0,1:T(4,128)(2,1)}), bf16[4,640,1152]{2,0,1:T(4,128)(2,1)}) %all-gather.6.cloned.1.call-update) | async-done | bytes 5898256 | tf_op jit(solution)/shard_map/all_gather | solution.py:127
  761.7 25.3 %fusion.110 = (bf16[4,640,1024]{2,0,1:T(4,128)(2,1)S(1)}, bf16[4,640,1024]{2,0,1:T(4,128)(2,1)S(1)}, bf16[4,640,1024]{2,0,1:T(4,128)(2,1)S(1)}, bf16[4,640,1024]{2,0,1:T(4,128)(2,1)S(1)}, bf16[4,640,1024]{2,0,1:T(4,128)(2,1)}) fusion(bf16[4,640,1152]{2,0,1:T(4,128)(2,1)} %all-gather.6.cloned.1.call-done), kind=kLoop, calls=%fused_computation.198 | loop fusion | bytes 52428800 | tf_op jit(solution)/shard_map/slice | solution.py:62
  787.0 8.6 fusion.28
  812.6 18.1 %multiply_reduce_fusion.2 = (f32[160]{0:T(256)S(1)}, f32[4,1024]{1,0:T(4,128)S(1)}, f32[4,1024]{1,0:T(4,128)S(1)}, f32[160]{0:T(256)S(1)}, f32[4,160,1024]{2,1,0:T(8,128)}) fusion(f32[4,1024]{1,0:T(4,128)S(1)} %get-tuple-element.115, f32[4,1024]{1,0:T(4,128)S(1)} %get-tuple-element.114, f32[160]{0:T(256)S(1)} %copy-done.24, ...), kind=kOutput, calls=%fused_computation.96 | convolution fusion | flops 4248690176 | bytes 32550016 | tf_op jit(solution)/shard_map/sml,mc->scl/dot_general | solution.py:132
  830.8 15.4 %all-reduce.6 = (f32[4,1,1024]{2,0,1:T(4,128)S(1)}, f32[4,1,1024]{2,0,1:T(4,128)S(1)}) all-reduce(f32[4,1,1024]{2,0,1:T(4,128)S(1)} %bitcast.202, f32[4,1,1024]{2,0,1:T(4,128)S(1)} %bitcast.203), channel_id=1, replica_groups=mesh['batch'=4,'seq'=2,'ch'=4] {'ch'}, use_global_device_ids=true, to_apply=%region_22.23 | all-reduce | flops 8192 | bytes 65536 | tf_op jit(solution)/shard_map/psum | solution.py:33
  853.2 9.4 convolution_bitcast_fusion
  862.6 25.4 %copy.67 = f32[4,1280,1024]{2,0,1:T(4,128)} copy(f32[4,1280,1024]{1,2,0:T(8,128)} %convolution_bitcast_fusion) | data formatting | bytes 41943040 | tf_op jit(solution)/shard_map/shl,hd->sdl/transpose | solution.py:110
  888.9 8.5 convolution_bitcast_fusion.3
  897.4 12.0 fusion.74
  914.7 8.1 fusion.93
  923.9 12.3 fusion.17
  936.2 17.4 %all-reduce.5 = (f32[4,1,1024]{2,0,1:T(4,128)S(1)}, f32[4,1,1024]{2,0,1:T(4,128)S(1)}) all-reduce(f32[4,1,1024]{2,0,1:T(4,128)S(1)} %bitcast.198, f32[4,1,1024]{2,0,1:T(4,128)S(1)} %bitcast.199), channel_id=1, replica_groups=mesh['batch'=4,'seq'=2,'ch'=4] {'ch'}, use_global_device_ids=true, to_apply=%region_26.27 | all-reduce | flops 8192 | bytes 65536 | tf_op jit(solution)/shard_map/psum | solution.py:33
  953.7 340.3 %all-reduce.20.cloned.1.call-done = f32[4,1280,1024]{2,0,1:T(4,128)} async-done(((f32[4,1280,1024]{2,0,1:T(4,128)}), f32[4,1280,1024]{2,0,1:T(4,128)}) %all-reduce.20.cloned.1.call-update) | async-done | bytes 20971536
  1299.7 6.9 convert_reduce_fusion.1
  1306.6 30.6 %all-reduce.3 = (f32[320]{0:T(512)}, f32[320]{0:T(512)}, f32[160]{0:T(256)}, f32[160]{0:T(256)}, f32[160]{0:T(256)}, /*index=5*/f32[160]{0:T(256)}, f32[160]{0:T(256)}, f32[160]{0:T(256)}, f32[320]{0:T(512)}) all-reduce(f32[320]{0:T(512)S(1)} %get-tuple-element.42, ...), channel_id=1, replica_groups=mesh['batch'=4,'seq'=2,'ch'=4] {'batch','seq'}, use_global_device_ids=true, to_apply=%region_28.29 | all-reduce | flops 1920 | bytes 15360 | tf_op jit(solution)/shard_map/psum | solution.py:157
  1337.2 50.5 %all-reduce.22.cloned.1.call-done = (f32[320,640]{1,0:T(8,128)}, f32[5,160,640]{2,1,0:T(8,128)}, f32[160,1280]{1,0:T(8,128)}) async-done(((f32[320,640]{1,0:T(8,128)}, f32[5,160,640]{2,1,0:T(8,128)}, f32[160,1280]{1,0:T(8,128)}), (f32[320,640]{1,0:T(8,128)}, f32[5,160,640]{2,1,0:T(8,128)}, f32[160,1280]{1,0:T(8,128)})) %all-reduce.22.cloned.1.call-update) | async-done | bytes 3686416 | tf_op jit(solution)/shard_map/psum | solution.py:157
  (145 shorter events, 89.6 us)
Async XLA Ops:
  7.2 306.6 %copy-start = (bf16[5,160,640]{2,1,0:T(8,128)(2,1)S(1)}, bf16[5,160,640]{2,1,0:T(8,128)(2,1)}, u32[]{:S(2)}) copy-start(bf16[5,160,640]{2,1,0:T(8,128)(2,1)} %param.23) | copy-start | bytes 3072004
  7.2 20.4 %copy-start.28 = (f32[320]{0:T(512)S(1)}, f32[320]{0:T(512)}, u32[]{:S(2)}) copy-start(f32[320]{0:T(512)} %param.17) | copy-start | bytes 3844
  7.2 20.4 %copy-start.34 = (f32[320]{0:T(512)S(1)}, f32[320]{0:T(512)}, u32[]{:S(2)}) copy-start(f32[320]{0:T(512)} %param.18) | copy-start | bytes 3844
  7.2 261.1 %all-reduce.16.cloned.1.call-start = ((), (), s32[]{:S(2)}) async-start(), calls=%async_computation.3 | async-start | bytes 20971520
  27.6 14.7 %copy-start.18 = (f32[4,1024]{1,0:T(4,128)}, f32[4,1024]{1,0:T(4,128)S(1)}, u32[]{:S(2)}) copy-start(f32[4,1024]{1,0:T(4,128)S(1)} %get-tuple-element.116) | copy-start | bytes 49156
  27.6 14.7 %copy-start.20 = (f32[4,1024]{1,0:T(4,128)}, f32[4,1024]{1,0:T(4,128)S(1)}, u32[]{:S(2)}) copy-start(f32[4,1024]{1,0:T(4,128)S(1)} %get-tuple-element.117) | copy-start | bytes 49156
  27.7 16.2 %copy-start.15 = (bf16[320,640]{1,0:T(8,128)(2,1)S(1)}, bf16[320,640]{1,0:T(8,128)(2,1)}, u32[]{:S(2)}) copy-start(bf16[320,640]{1,0:T(8,128)(2,1)} %param.19) | copy-start | bytes 1228804
  62.5 480.2 %all-reduce.18.cloned.1.call-start = ((), (), s32[]{:S(2)}) async-start(), calls=%async_computation.4 | async-start | bytes 20971520
  63.2 235.7 %collective-permute-start.2 = (s32[4,64]{1,0:T(4,128)S(1)}, s32[4,64]{1,0:T(4,128)S(1)}, u32[]{:S(2)}, u32[]{:S(2)}) collective-permute-start(s32[4,64]{1,0:T(4,128)S(1)} %get-tuple-element.112), channel_id=1, source_target_pairs={{4,0},{5,1},{6,2},{7,3},{12,8},{13,9},{14,10},{15,11},{20,16},{21,... | collective-permute-start | bytes 3080 | tf_op jit(solution)/shard_map/ppermute | solution.py:19
  64.5 234.4 %collective-permute-start = (s32[4,64]{1,0:T(4,128)S(1)}, s32[4,64]{1,0:T(4,128)S(1)}, u32[]{:S(2)}, u32[]{:S(2)}) collective-permute-start(s32[4,64]{1,0:T(4,128)S(1)} %get-tuple-element.113), channel_id=1, source_target_pairs={{0,4},{1,5},{2,6},{3,7},{8,12},{9,13},{10,14},{11,15},{16,20},{17,... | collective-permute-start | bytes 3080 | tf_op jit(solution)/shard_map/ppermute | solution.py:18
  68.8 203.3 %copy-start.23 = (f32[160]{0:T(256)S(1)}, f32[160]{0:T(256)}, u32[]{:S(2)}) copy-start(f32[160]{0:T(256)} %param.20) | copy-start | bytes 1924
  272.1 17.2 %copy-start.26 = (f32[160]{0:T(256)S(1)}, f32[160]{0:T(256)}, u32[]{:S(2)}) copy-start(f32[160]{0:T(256)} %param.21) | copy-start | bytes 1924
  272.1 17.2 %copy-start.32 = (f32[160]{0:T(256)S(1)}, f32[160]{0:T(256)}, u32[]{:S(2)}) copy-start(f32[160]{0:T(256)} %param.22) | copy-start | bytes 1924
  297.6 2.9 collective-permute-start.1
  299.0 10.4 collective-permute-start.3
  335.8 314.4 %all-gather.4.cloned.1.call-start = ((), (), s32[]{:S(2)}) async-start(), calls=%async_computation | async-start | bytes 13107200 | tf_op jit(solution)/shard_map/all_gather | solution.py:113
  336.5 209.9 %copy-start.25 = (f32[160]{0:T(256)S(1)}, f32[160]{0:T(256)}, u32[]{:S(2)}) copy-start(f32[160]{0:T(256)} %param.24) | copy-start | bytes 1924
  336.5 425.2 %all-gather.6.cloned.1.call-start = ((), (), s32[]{:S(2)}) async-start(), calls=%async_computation.1 | async-start | bytes 7372800 | tf_op jit(solution)/shard_map/all_gather | solution.py:127
  546.4 18.2 %copy-start.30 = (f32[160]{0:T(256)S(1)}, f32[160]{0:T(256)}, u32[]{:S(2)}) copy-start(f32[160]{0:T(256)} %param.25) | copy-start | bytes 1924
  546.4 18.2 %copy-start.37 = (f32[160]{0:T(256)S(1)}, f32[160]{0:T(256)}, u32[]{:S(2)}) copy-start(f32[160]{0:T(256)} %param.26) | copy-start | bytes 1924
  564.7 85.5 %copy-start.13 = (bf16[160,1280]{1,0:T(8,128)(2,1)S(1)}, bf16[160,1280]{1,0:T(8,128)(2,1)}, u32[]{:S(2)}) copy-start(bf16[160,1280]{1,0:T(8,128)(2,1)} %param.27) | copy-start | bytes 1228804
  683.5 4.4 collective-permute-start.5
  684.8 4.1 collective-permute-start.4
  694.6 220.1 %all-gather.8.cloned.1.call-start = ((), (), s32[]{:S(2)}) async-start(), calls=%async_computation.2 | async-start | bytes 6553600 | tf_op jit(solution)/shard_map/all_gather | solution.py:146
  787.0 12.9 copy-start.7
  853.1 440.9 %all-reduce.20.cloned.1.call-start = ((), (), s32[]{:S(2)}) async-start(), calls=%async_computation.5 | async-start | bytes 41943040
  888.0 499.6 %all-reduce.22.cloned.1.call-start = ((), (), s32[]{:S(2)}) async-start(), calls=%async_computation.6 | async-start | bytes 7372800 | tf_op jit(solution)/shard_map/psum | solution.py:157
  953.7 344.3 %copy-start.36 = (f32[320]{0:T(512)S(1)}, f32[320]{0:T(512)}, u32[]{:S(2)}) copy-start(f32[320]{0:T(512)} %param.28) | copy-start | bytes 3844
  1299.6 6.9 copy-start.31
  1299.6 6.9 copy-start.38
  1299.7 6.9 copy-start.39
  1387.6 6.1 copy-start.1
  (22 other events, 60.9 us)
Sparse Core Ops, SparseCore 0:
  62.6 205.6 all-reduce.15
  335.9 206.6 all-reduce.17
  544.5 105.6 all-gather.3
  694.8 66.8 all-gather.5
  853.3 61.3 all-gather.7
  918.1 375.9 all-reduce.19
  1297.9 89.6 all-reduce.21
where the time goes:
time: 1410 us; the launch traced here: 1400 us
  waiting for transfers between devices  947 us (67%)
  blocking collectives  129 us (9%)
  local copies, waits for them, and re-layouts  115 us (8%)
  matrix products  95.6 us (7%)
  other arithmetic  86.6 us (6%)
  between operations  16.2 us (1%)
    unnamed x10, waiting for transfers between devices  747 us
    psum x6, blocking collectives, channel_sums(): return lax.psum((first, second), 'ch')  98.3 us
    all_gather x1, waiting for transfers between devices, local(): piece = lax.all_gather(cotangent, 'ch', axis=1, tiled=True)  76.4 us
    all_gather x1, waiting for transfers between devices, local(): piece = lax.all_gather(wide_grad, 'ch', axis=1, tiled=True)  66.8 us
    psum x1, waiting for transfers between devices, local(): lax.psum((grad_norm0_gain, grad_norm0_shift, grad_weight, grad_b_inner, g...  50.5 us
    psum x1, blocking collectives, local(): lax.psum((grad_norm0_gain, grad_norm0_shift, grad_weight, grad_b_inner, g...  30.6 us
    unnamed x90, local copies, waits for them, and re-layouts  30.3 us
  transfers between devices with their start and end apart: 13, of which 8 were waited for; matrix products, arithmetic and copies ran while one was open for 9% of the time, Pallas kernels for 0%

commit v1 on v0

--- a/solution.py
+++ b/solution.py
@@ -155,21 +155,24 @@
         cotangent.astype(jnp.float32) + normalize_back(grad_normed0, unit0, scale0, norm0_gain)
     ).astype(jnp.bfloat16)
     totals = lax.psum(
-        (
-            grad_norm0_gain,
-            grad_norm0_shift,
-            grad_weight,
-            grad_b_inner,
-            grad_norm1_gain,
-            grad_norm1_shift,
-            grad_kernel,
-            grad_b_conv,
-            grad_norm2_gain,
-            grad_norm2_shift,
-            grad_w_outer,
-            grad_b_outer,
+        lax.psum(
+            (
+                grad_norm0_gain,
+                grad_norm0_shift,
+                grad_weight,
+                grad_b_inner,
+                grad_norm1_gain,
+                grad_norm1_shift,
+                grad_kernel,
+                grad_b_conv,
+                grad_norm2_gain,
+                grad_norm2_shift,
+                grad_w_outer,
+                grad_b_outer,
+            ),
+            "seq",
         ),
-        ("batch", "seq"),
+        "batch",
     )
     return (
         output,

time: 1410 us -> 1500 us (1.064)
  waiting for transfers between devices: 947 us -> 1050 us
    psum x0 -> x1, waiting for transfers between devices: none -> 107 us  [local(): lax.psum(lax.psum((grad_norm0_gain, grad_norm0_shift, grad_weight, grad_b...]
    psum x1, waiting for transfers between devices: 50.5 us -> 0.02 us  [local(): lax.psum((grad_norm0_gain, grad_norm0_shift, grad_weight, grad_b_inner, g...]
    all_gather x1, waiting for transfers between devices: 5.33 us -> 41.7 us  [local(): piece = lax.all_gather(grad_inner, 'ch', axis=1, tiled=True)]
    psum x1, blocking collectives: 30.6 us -> 3.37 us  [local(): lax.psum((grad_norm0_gain, grad_norm0_shift, grad_weight, grad_b_inner, g...]
    psum x0 -> x1, blocking collectives: none -> 20.4 us  [local(): lax.psum(lax.psum((grad_norm0_gain, grad_norm0_shift, grad_weight, grad_b...]
    unnamed x10 -> x11, waiting for transfers between devices: 747 us -> 753 us
    unnamed x90 -> x94, local copies, waits for them, and re-layouts: 30.3 us -> 30.1 us
  transfers between devices with their start and end apart: 13 -> 14, of which waited for: 8 -> 8; matrix products, arithmetic and copies ran while one was open for 9% -> 8% of each run, Pallas kernels for 0% -> 0%
where the time goes in v1:
time: 1500 us; the launch traced here: 1490 us
  waiting for transfers between devices  1050 us (70%)
  blocking collectives  121 us (8%)
  local copies, waits for them, and re-layouts  115 us (8%)
  matrix products  95.1 us (6%)
  other arithmetic  86.6 us (6%)
  between operations  16.3 us (1%)
    unnamed x11, waiting for transfers between devices  753 us
    psum x1, waiting for transfers between devices, local(): lax.psum(lax.psum((grad_norm0_gain, grad_norm0_shift, grad_weight, grad_b...  107 us
    psum x6, blocking collectives, channel_sums(): return lax.psum((first, second), 'ch')  96.9 us
    all_gather x1, waiting for transfers between devices, local(): piece = lax.all_gather(cotangent, 'ch', axis=1, tiled=True)  76.8 us
    all_gather x1, waiting for transfers between devices, local(): piece = lax.all_gather(wide_grad, 'ch', axis=1, tiled=True)  66.8 us
    all_gather x1, waiting for transfers between devices, local(): piece = lax.all_gather(grad_inner, 'ch', axis=1, tiled=True)  41.7 us
    unnamed x94, local copies, waits for them, and re-layouts  30.1 us
  transfers between devices with their start and end apart: 14, of which 8 were waited for; matrix products, arithmetic and copies ran while one was open for 8% of the time, Pallas kernels for 0%

profile of v1, /device:TPU:0, one launch (start us, length us, event | category | flops | bytes accessed | tf_op | source)
XLA Modules:
  0.0 1492.0 jit_solution(13114289917320067908)
XLA Ops:
  9.8 17.8 %all-reduce.8 = (f32[4,1,1024]{2,0,1:T(4,128)S(1)}, f32[4,1,1024]{2,0,1:T(4,128)S(1)}) all-reduce(f32[4,1,1024]{2,0,1:T(4,128)S(1)} %bitcast.199, f32[4,1,1024]{2,0,1:T(4,128)S(1)} %bitcast.198), channel_id=1, replica_groups=mesh['batch'=4,'seq'=2,'ch'=4] {'ch'}, use_global_device_ids=true, to_apply=%region_3.0 | all-reduce | flops 8192 | bytes 65536 | tf_op jit(solution)/shard_map/psum | solution.py:33
  27.7 14.6 multiply_convert_fusion
  49.5 12.9 copy.63
  68.8 199.5 %all-reduce.19.cloned.1.call-done = f32[4,640,1024]{2,0,1:T(4,128)} async-done(((f32[4,640,1024]{2,0,1:T(4,128)}), f32[4,640,1024]{2,0,1:T(4,128)}) %all-reduce.19.cloned.1.call-update) | async-done | bytes 10485776
  273.5 15.7 %all-reduce.7 = (f32[4,1,1024]{2,0,1:T(4,128)S(1)}, f32[4,1,1024]{2,0,1:T(4,128)S(1)}) all-reduce(f32[4,1,1024]{2,0,1:T(4,128)S(1)} %bitcast.195, f32[4,1,1024]{2,0,1:T(4,128)S(1)} %bitcast.194), channel_id=1, replica_groups=mesh['batch'=4,'seq'=2,'ch'=4] {'ch'}, use_global_device_ids=true, to_apply=%region_8.0 | all-reduce | flops 8192 | bytes 65536 | tf_op jit(solution)/shard_map/psum | solution.py:33
  289.3 8.2 multiply_convert_fusion.4
  302.5 7.1 bitcast_dynamic-update-slice_fusion.1
  314.1 9.1 convolution_bitcast_fusion.2
  323.2 12.9 copy.65
  336.9 206.1 %all-reduce.21.cloned.1.call-done = f32[4,640,1024]{2,0,1:T(4,128)} async-done(((f32[4,640,1024]{2,0,1:T(4,128)}), f32[4,640,1024]{2,0,1:T(4,128)}) %all-reduce.21.cloned.1.call-update) | async-done | bytes 10485776
  548.2 16.4 %all-reduce.6 = (f32[4,1,1024]{2,0,1:T(4,128)S(1)}, f32[4,1,1024]{2,0,1:T(4,128)S(1)}) all-reduce(f32[4,1,1024]{2,0,1:T(4,128)S(1)} %bitcast.197, f32[4,1,1024]{2,0,1:T(4,128)S(1)} %bitcast.196), channel_id=1, replica_groups=mesh['batch'=4,'seq'=2,'ch'=4] {'ch'}, use_global_device_ids=true, to_apply=%region_13.14 | all-reduce | flops 8192 | bytes 65536 | tf_op jit(solution)/shard_map/psum | solution.py:33
  564.7 9.1 multiply_convert_fusion.3
  573.8 76.8 %all-gather.4.cloned.1.call-done = bf16[4,1280,1024]{2,1,0:T(8,128)(2,1)} async-done(((bf16[4,320,1024]{2,1,0:T(8,128)(2,1)}), bf16[4,1280,1024]{2,1,0:T(8,128)(2,1)}) %all-gather.4.cloned.1.call-update) | async-done | bytes 10485776 | tf_op jit(solution)/shard_map/all_gather | solution.py:113
  650.5 12.3 multiply_reduce_fusion.1
  662.8 15.4 %all-reduce.5 = (f32[4,1,1024]{2,0,1:T(4,128)S(1)}, f32[4,1,1024]{2,0,1:T(4,128)S(1)}) all-reduce(f32[4,1,1024]{2,0,1:T(4,128)S(1)} %bitcast.202, f32[4,1,1024]{2,0,1:T(4,128)S(1)} %bitcast.203), channel_id=1, replica_groups=mesh['batch'=4,'seq'=2,'ch'=4] {'ch'}, use_global_device_ids=true, to_apply=%region_18.19 | all-reduce | flops 8192 | bytes 65536 | tf_op jit(solution)/shard_map/psum | solution.py:33
  695.2 66.8 %all-gather.6.cloned.1.call-done = bf16[4,640,1152]{2,0,1:T(4,128)(2,1)} async-done(((bf16[4,160,1152]{2,0,1:T(4,128)(2,1)}), bf16[4,640,1152]{2,0,1:T(4,128)(2,1)}) %all-gather.6.cloned.1.call-update) | async-done | bytes 5898256 | tf_op jit(solution)/shard_map/all_gather | solution.py:127
  761.9 25.5 %fusion.110 = (bf16[4,640,1024]{2,0,1:T(4,128)(2,1)S(1)}, bf16[4,640,1024]{2,0,1:T(4,128)(2,1)S(1)}, bf16[4,640,1024]{2,0,1:T(4,128)(2,1)S(1)}, bf16[4,640,1024]{2,0,1:T(4,128)(2,1)S(1)}, bf16[4,640,1024]{2,0,1:T(4,128)(2,1)}) fusion(bf16[4,640,1152]{2,0,1:T(4,128)(2,1)} %all-gather.6.cloned.1.call-done), kind=kLoop, calls=%fused_computation.198 | loop fusion | bytes 52428800 | tf_op jit(solution)/shard_map/slice | solution.py:62
  787.4 8.6 fusion.28
  813.0 18.1 %multiply_reduce_fusion.2 = (f32[160]{0:T(256)S(1)}, f32[4,1024]{1,0:T(4,128)S(1)}, f32[4,1024]{1,0:T(4,128)S(1)}, f32[160]{0:T(256)S(1)}, f32[4,160,1024]{2,1,0:T(8,128)}) fusion(f32[4,1024]{1,0:T(4,128)S(1)} %get-tuple-element.127, f32[4,1024]{1,0:T(4,128)S(1)} %get-tuple-element.126, f32[160]{0:T(256)S(1)} %copy-done.24, ...), kind=kOutput, calls=%fused_computation.96 | convolution fusion | flops 4248690176 | bytes 32550016 | tf_op jit(solution)/shard_map/sml,mc->scl/dot_general | solution.py:132
  831.1 15.4 %all-reduce.4 = (f32[4,1,1024]{2,0,1:T(4,128)S(1)}, f32[4,1,1024]{2,0,1:T(4,128)S(1)}) all-reduce(f32[4,1,1024]{2,0,1:T(4,128)S(1)} %bitcast.204, f32[4,1,1024]{2,0,1:T(4,128)S(1)} %bitcast.205), channel_id=1, replica_groups=mesh['batch'=4,'seq'=2,'ch'=4] {'ch'}, use_global_device_ids=true, to_apply=%region_22.23 | all-reduce | flops 8192 | bytes 65536 | tf_op jit(solution)/shard_map/psum | solution.py:33
  853.7 8.6 convolution_bitcast_fusion.3
  862.4 10.9 fusion.74
  873.3 41.7 %all-gather.8.cloned.1.call-done = bf16[4,640,1024]{2,0,1:T(4,128)(2,1)} async-done(((bf16[4,160,1024]{2,0,1:T(4,128)(2,1)}), bf16[4,640,1024]{2,0,1:T(4,128)(2,1)}) %all-gather.8.cloned.1.call-update) | async-done | bytes 5242896 | tf_op jit(solution)/shard_map/all_gather | solution.py:146
  915.1 8.1 fusion.93
  924.1 10.0 convolution_bitcast_fusion
  934.2 25.5 %copy.67 = f32[4,1280,1024]{2,0,1:T(4,128)} copy(f32[4,1280,1024]{1,2,0:T(8,128)} %convolution_bitcast_fusion) | data formatting | bytes 41943040 | tf_op jit(solution)/shard_map/shl,hd->sdl/transpose | solution.py:110
  961.1 12.2 fusion.17
  973.3 16.3 %all-reduce.3 = (f32[4,1,1024]{2,0,1:T(4,128)S(1)}, f32[4,1,1024]{2,0,1:T(4,128)S(1)}) all-reduce(f32[4,1,1024]{2,0,1:T(4,128)S(1)} %bitcast.200, f32[4,1,1024]{2,0,1:T(4,128)S(1)} %bitcast.201), channel_id=1, replica_groups=mesh['batch'=4,'seq'=2,'ch'=4] {'ch'}, use_global_device_ids=true, to_apply=%region_26.27 | all-reduce | flops 8192 | bytes 65536 | tf_op jit(solution)/shard_map/psum | solution.py:33
  989.7 346.0 %all-reduce.23.cloned.1.call-done = f32[4,1280,1024]{2,0,1:T(4,128)} async-done(((f32[4,1280,1024]{2,0,1:T(4,128)}), f32[4,1280,1024]{2,0,1:T(4,128)}) %all-reduce.23.cloned.1.call-update) | async-done | bytes 20971536
  1341.3 6.9 convert_reduce_fusion.1
  1351.6 20.4 %all-reduce.9 = (f32[320]{0:T(512)}, f32[320]{0:T(512)}, f32[160]{0:T(256)}, f32[160]{0:T(256)}, f32[160]{0:T(256)}, /*index=5*/f32[160]{0:T(256)}, f32[160]{0:T(256)}, f32[160]{0:T(256)}, f32[320]{0:T(512)}) all-reduce(f32[320]{0:T(512)S(1)} %get-tuple-element.84, ...), channel_id=1, replica_groups=mesh['batch'=4,'seq'=2,'ch'=4] {'batch'}, use_global_device_ids=true, to_apply=%region_29.30 | all-reduce | flops 1920 | bytes 15360 | tf_op jit(solution)/shard_map/psum | solution.py:157
  1372.0 106.8 %all-reduce.25.cloned.1.call-done = (f32[320,640]{1,0:T(8,128)}, f32[5,160,640]{2,1,0:T(8,128)}, f32[160,1280]{1,0:T(8,128)}) async-done(((f32[320,640]{1,0:T(8,128)}, f32[5,160,640]{2,1,0:T(8,128)}, f32[160,1280]{1,0:T(8,128)}), (f32[320,640]{1,0:T(8,128)}, f32[5,160,640]{2,1,0:T(8,128)}, f32[160,1280]{1,0:T(8,128)})) %all-reduce.25.cloned.1.call-update) | async-done | bytes 3686416 | tf_op jit(solution)/shard_map/psum | solution.py:157
  (154 shorter events, 94.2 us)
Async XLA Ops:
  7.2 306.9 %copy-start = (bf16[5,160,640]{2,1,0:T(8,128)(2,1)S(1)}, bf16[5,160,640]{2,1,0:T(8,128)(2,1)}, u32[]{:S(2)}) copy-start(bf16[5,160,640]{2,1,0:T(8,128)(2,1)} %param.23) | copy-start | bytes 3072004
  7.2 20.4 %copy-start.28 = (f32[320]{0:T(512)S(1)}, f32[320]{0:T(512)}, u32[]{:S(2)}) copy-start(f32[320]{0:T(512)} %param.17) | copy-start | bytes 3844
  7.2 20.4 %copy-start.34 = (f32[320]{0:T(512)S(1)}, f32[320]{0:T(512)}, u32[]{:S(2)}) copy-start(f32[320]{0:T(512)} %param.18) | copy-start | bytes 3844
  7.2 261.0 %all-reduce.19.cloned.1.call-start = ((), (), s32[]{:S(2)}) async-start(), calls=%async_computation.3 | async-start | bytes 20971520
  27.6 14.7 copy-start.18
  27.6 14.7 copy-start.20
  27.7 16.1 %copy-start.15 = (bf16[320,640]{1,0:T(8,128)(2,1)S(1)}, bf16[320,640]{1,0:T(8,128)(2,1)}, u32[]{:S(2)}) copy-start(bf16[320,640]{1,0:T(8,128)(2,1)} %param.19) | copy-start | bytes 1228804
  62.4 480.5 %all-reduce.21.cloned.1.call-start = ((), (), s32[]{:S(2)}) async-start(), calls=%async_computation.4 | async-start | bytes 20971520
  63.2 235.7 %collective-permute-start.2 = (s32[4,64]{1,0:T(4,128)S(1)}, s32[4,64]{1,0:T(4,128)S(1)}, u32[]{:S(2)}, u32[]{:S(2)}) collective-permute-start(s32[4,64]{1,0:T(4,128)S(1)} %get-tuple-element.124), channel_id=1, source_target_pairs={{4,0},{5,1},{6,2},{7,3},{12,8},{13,9},{14,10},{15,11},{20,16},{21,... | collective-permute-start | bytes 3080 | tf_op jit(solution)/shard_map/ppermute | solution.py:19
  64.5 234.4 %collective-permute-start = (s32[4,64]{1,0:T(4,128)S(1)}, s32[4,64]{1,0:T(4,128)S(1)}, u32[]{:S(2)}, u32[]{:S(2)}) collective-permute-start(s32[4,64]{1,0:T(4,128)S(1)} %get-tuple-element.125), channel_id=1, source_target_pairs={{0,4},{1,5},{2,6},{3,7},{8,12},{9,13},{10,14},{11,15},{16,20},{17,... | collective-permute-start | bytes 3080 | tf_op jit(solution)/shard_map/ppermute | solution.py:18
  68.8 203.3 %copy-start.23 = (f32[160]{0:T(256)S(1)}, f32[160]{0:T(256)}, u32[]{:S(2)}) copy-start(f32[160]{0:T(256)} %param.20) | copy-start | bytes 1924
  272.0 17.2 %copy-start.26 = (f32[160]{0:T(256)S(1)}, f32[160]{0:T(256)}, u32[]{:S(2)}) copy-start(f32[160]{0:T(256)} %param.21) | copy-start | bytes 1924
  272.0 17.2 %copy-start.32 = (f32[160]{0:T(256)S(1)}, f32[160]{0:T(256)}, u32[]{:S(2)}) copy-start(f32[160]{0:T(256)} %param.22) | copy-start | bytes 1924
  297.6 3.2 collective-permute-start.1
  299.0 10.7 collective-permute-start.3
  336.1 314.4 %all-gather.4.cloned.1.call-start = ((), (), s32[]{:S(2)}) async-start(), calls=%async_computation | async-start | bytes 13107200 | tf_op jit(solution)/shard_map/all_gather | solution.py:113
  336.8 209.9 %copy-start.25 = (f32[160]{0:T(256)S(1)}, f32[160]{0:T(256)}, u32[]{:S(2)}) copy-start(f32[160]{0:T(256)} %param.24) | copy-start | bytes 1924
  336.8 425.1 %all-gather.6.cloned.1.call-start = ((), (), s32[]{:S(2)}) async-start(), calls=%async_computation.1 | async-start | bytes 7372800 | tf_op jit(solution)/shard_map/all_gather | solution.py:127
  546.8 17.9 %copy-start.30 = (f32[160]{0:T(256)S(1)}, f32[160]{0:T(256)}, u32[]{:S(2)}) copy-start(f32[160]{0:T(256)} %param.25) | copy-start | bytes 1924
  546.8 17.9 %copy-start.37 = (f32[160]{0:T(256)S(1)}, f32[160]{0:T(256)}, u32[]{:S(2)}) copy-start(f32[160]{0:T(256)} %param.26) | copy-start | bytes 1924
  564.7 85.9 %copy-start.13 = (bf16[160,1280]{1,0:T(8,128)(2,1)S(1)}, bf16[160,1280]{1,0:T(8,128)(2,1)}, u32[]{:S(2)}) copy-start(bf16[160,1280]{1,0:T(8,128)(2,1)} %param.27) | copy-start | bytes 1228804
  683.8 4.4 collective-permute-start.5
  685.1 4.1 collective-permute-start.4
  694.9 220.1 %all-gather.8.cloned.1.call-start = ((), (), s32[]{:S(2)}) async-start(), calls=%async_computation.2 | async-start | bytes 6553600 | tf_op jit(solution)/shard_map/all_gather | solution.py:146
  787.4 12.9 copy-start.7
  851.4 11.0 slice-start
  853.5 106.5 %all-reduce.27.cloned.1.call-start = ((), (), s32[]{:S(2)}) async-start(), calls=%async_computation.7 | async-start | bytes 7372800 | tf_op jit(solution)/shard_map/psum | solution.py:158
  853.7 8.7 slice-start.1
  923.2 412.5 %all-reduce.23.cloned.1.call-start = ((), (), s32[]{:S(2)}) async-start(), calls=%async_computation.5 | async-start | bytes 41943040
  959.7 519.1 %all-reduce.25.cloned.1.call-start = ((), (), s32[]{:S(2)}) async-start(), calls=%async_computation.6 | async-start | bytes 7372800 | tf_op jit(solution)/shard_map/psum | solution.py:157
  989.7 349.9 %copy-start.36 = (f32[320]{0:T(512)S(1)}, f32[320]{0:T(512)}, u32[]{:S(2)}) copy-start(f32[320]{0:T(512)} %param.28) | copy-start | bytes 3844
  1341.3 6.9 copy-start.39
  (25 other events, 81.6 us)
Sparse Core Ops, SparseCore 0:
  62.5 205.6 all-reduce.18
  336.2 206.7 all-reduce.20
  544.8 105.6 all-gather.3
  695.0 66.8 all-gather.5
  853.6 61.4 all-gather.7
  923.3 24.4 all-reduce.26
  959.8 375.8 all-reduce.22
  1338.3 140.5 all-reduce.24
